TPU v7x, 256 devices: a whole 4x4x8 slice. The times are simulated.
256 devices in a mesh: seq: 32 (over x, y, core), head: 8 (over z).
Axes of the slice: x: 4, y: 4, z: 8, core: 2. Of those that a mesh axis runs over, the one named last changes fastest.
Arguments:
- queries: bfloat16 [1, 8192, 4096], P(None, 'seq', 'head'), may hold values from -6 to 6
- keys: bfloat16 [1, 8192, 4096], P(None, 'seq', 'head'), may hold values from -6 to 6
- values: bfloat16 [1, 8192, 4096], P(None, 'seq', 'head'), may hold values from -6 to 6
- out_weight: bfloat16 [4096, 4096], P('head'), may hold values from -0.09375 to 0.09375
- out_grad: bfloat16 [1, 8192, 4096], P(None, 'seq', 'head'), may hold values from -6 to 6
- block_doc: int32 [1, 32], replicated, may hold values from 0 to 2, never falling along the last dimension, each value on 1 to 24 neighbouring positions
Outputs:
- context: bfloat16 [1, 8192, 4096], P(None, 'seq', 'head')
- query_grad: bfloat16 [1, 8192, 4096], P(None, 'seq', 'head')
- key_grad: bfloat16 [1, 8192, 4096], P(None, 'seq', 'head')
- value_grad: bfloat16 [1, 8192, 4096], P(None, 'seq', 'head')
- weight_grad: bfloat16 [4096, 4096], P('head', 'seq')
Inputs may be any that keep to these rules, and one draw needn't show every extreme that they name: `block_doc`: document numbers never fall along a pack, every document holds whole leaf blocks, and one document covers exactly 24 blocks.
All inputs are finite; a program needn't handle non-finite values.
Results may differ from a plain program's by a relative error of at most 0.019.
Values may be sent and summed in bfloat16 or wider, within the bound.
No kernel may reach another device: no remote copies, remote signals or barrier semaphores. Data moves between devices by JAX's collectives and lax.ppermute only.
A program may use at most 128 MiB of HBM per device.

v0:
```python
import functools
import math

import jax
import jax.numpy as jnp
from jax import lax
from jax.experimental import pallas as pl
from jax.experimental.pallas import tpu as pltpu
from jax.sharding import PartitionSpec as P

DH = 128
F32 = jnp.float32
BF16 = jnp.bfloat16
HOPS = (1, 2, 6, 8, 24)


def swapped(value, level_num):
    count = lax.axis_size("seq")
    return lax.ppermute(value, "seq", [(i, i ^ HOPS[level_num]) for i in range(count)])


def mm(a, b, dims):
    return lax.dot_general(a, b, (dims, ((), ())), preferred_element_type=F32)


def pool_matrix(rows):
    r = lax.broadcasted_iota(jnp.int32, (rows // 2, rows), 0)
    c = lax.broadcasted_iota(jnp.int32, (rows // 2, rows), 1)
    return jnp.where((c >> 1) == r, 0.5, 0.0).astype(BF16)


def spread_matrix(rows):
    r = lax.broadcasted_iota(jnp.int32, (rows, rows // 2), 0)
    c = lax.broadcasted_iota(jnp.int32, (rows, rows // 2), 1)
    return jnp.where((r >> 1) == c, 0.5, 0.0).astype(BF16)


def pool_into(out_ref, bit, mine, other):
    rows = mine.shape[0]
    half = rows // 2
    mat = pool_matrix(rows)
    low = mm(mat, mine, ((1,), (0,))).astype(BF16)
    high = mm(mat, other, ((1,), (0,))).astype(BF16)
    out_ref[pl.ds(pl.multiple_of(bit * half, half), half), :] = low
    out_ref[pl.ds(pl.multiple_of((1 - bit) * half, half), half), :] = high


def pool_kernel(level_num, place_ref, mine_ref, other_ref, out_ref):
    bit = (place_ref[0] >> level_num) & 1
    pool_into(out_ref, bit, mine_ref[...], other_ref[...])


def pool_first_kernel(place_ref, key_ref, value_ref, other_key_ref, other_value_ref, out_ref):
    core = place_ref[0] & 1

    @pl.when(core == 0)
    def _():
        pool_into(out_ref, core, key_ref[...], other_key_ref[...])

    @pl.when(core == 1)
    def _():
        pool_into(out_ref, core, value_ref[...], other_value_ref[...])


SMEM = pl.BlockSpec(memory_space=pltpu.SMEM)
VMEM = pl.BlockSpec(memory_space=pltpu.VMEM)


def whole_call(kernel, place, args, outs, scratch=(), name=None):
    return pl.pallas_call(
        kernel,
        in_specs=[SMEM] + [VMEM] * len(args),
        out_specs=[VMEM] * len(outs),
        out_shape=[jax.ShapeDtypeStruct(s, d) for s, d in outs],
        scratch_shapes=list(scratch),
        name=name,
    )(place, *args)


def gather_columns(core, dest_k, dest_v, firsts, mine, other):
    rows = firsts[0].shape[0]
    dest_k[0:rows, :] = firsts[0][...]
    dest_k[rows : 2 * rows, :] = firsts[1][...]
    dest_v[0:rows, :] = firsts[2][...]
    dest_v[rows : 2 * rows, :] = firsts[3][...]

    @pl.when(core == 0)
    def _():
        for i in range(len(mine)):
            dest_k[(2 + i) * rows : (3 + i) * rows, :] = mine[i][...]
            dest_v[(2 + i) * rows : (3 + i) * rows, :] = other[i][...]

    @pl.when(core == 1)
    def _():
        for i in range(len(mine)):
            dest_k[(2 + i) * rows : (3 + i) * rows, :] = other[i][...]
            dest_v[(2 + i) * rows : (3 + i) * rows, :] = mine[i][...]


def forward_kernel(scaling, n_up, place_ref, weight_ref, query_ref, *refs):
    firsts, mine, other = refs[:4], refs[4 : 4 + n_up], refs[4 + n_up : 4 + 2 * n_up]
    context_ref, prob_ref, kcol_ref, vcol_ref = refs[4 + 2 * n_up :]
    gather_columns(place_ref[0] & 1, kcol_ref, vcol_ref, firsts, mine, other)
    col_weight = weight_ref[...]
    scores = mm(query_ref[...], kcol_ref[...], ((1,), (1,))) * scaling
    masked = jnp.where(col_weight > 0.0, scores, -jnp.inf)
    row_max = jnp.max(masked, axis=-1, keepdims=True)
    weights = col_weight * jnp.exp(masked - row_max)
    total = jnp.sum(weights, axis=-1, keepdims=True)
    prob = (weights * (1.0 / total)).astype(BF16)
    prob_ref[0] = prob
    context_ref[...] = mm(prob, vcol_ref[...], ((1,), (0,))).astype(BF16)


def backward_kernel(scaling, n_up, place_ref, query_ref, prob_ref, context_ref, grad_ref, *refs):
    kcol_ref, vcol_ref = refs[:2]
    dq_ref, own_k, own_v, sib_k, sib_v, keep_ref, send_ref = refs[2:]
    core = place_ref[0] & 1
    rows = query_ref.shape[0]
    grad = grad_ref[...]
    prob = prob_ref[0]
    delta = jnp.sum(grad.astype(F32) * context_ref[...].astype(F32), axis=-1, keepdims=True)
    prob_grad = mm(grad, vcol_ref[...], ((1,), (1,)))
    score_grad = (prob.astype(F32) * (prob_grad - delta)).astype(BF16)
    dq_ref[...] = (mm(score_grad, kcol_ref[...], ((1,), (0,))) * scaling).astype(BF16)
    dk = mm(score_grad, query_ref[...], ((0,), (0,))) * scaling
    dv = mm(prob, grad, ((0,), (0,)))
    own_k[...] = dk[:rows]
    own_v[...] = dv[:rows]
    sib_k[...] = dk[rows : 2 * rows]
    sib_v[...] = dv[rows : 2 * rows]
    up_k = dk[2 * rows :].reshape(n_up, rows, DH)
    up_v = dv[2 * rows :].reshape(n_up, rows, DH)

    @pl.when(core == 0)
    def _():
        keep_ref[...] = up_k
        send_ref[...] = up_v.astype(BF16)

    @pl.when(core == 1)
    def _():
        keep_ref[...] = up_v
        send_ref[...] = up_k.astype(BF16)


def spread_half(hi_ref, lo_ref, bit):
    rows = hi_ref.shape[0]
    half = rows // 2
    mat = spread_matrix(rows)
    part = pl.ds(pl.multiple_of(bit * half, half), half)
    return mm(mat, hi_ref[part, :], ((1,), (0,))) + mm(mat, lo_ref[part, :], ((1,), (0,)))


def split_held(hi_ref, lo_ref, held):
    hi = held.astype(BF16)
    hi_ref[...] = hi
    lo_ref[...] = (held - hi.astype(F32)).astype(BF16)


def climb_kernel(level_num, place_ref, held_ref, back_ref, keep_ref, recv_ref, send_ref, own_ref, hi_ref, lo_ref):
    bit = (place_ref[0] >> level_num) & 1
    split_held(hi_ref, lo_ref, held_ref[...] + back_ref[...].astype(F32))
    other = spread_half(hi_ref, lo_ref, 1 - bit)
    send_ref[...] = (keep_ref[0] + recv_ref[0].astype(F32) + other).astype(BF16)
    own_ref[...] = spread_half(hi_ref, lo_ref, bit)


def leaf_kernel(
    place_ref, held_ref, back_ref, own_k, own_v, sib_k, sib_v,
    send_k, send_v, total_k, total_v, hi_ref, lo_ref,
):
    core = place_ref[0] & 1
    split_held(hi_ref, lo_ref, held_ref[...] + back_ref[...].astype(F32))
    other = spread_half(hi_ref, lo_ref, 1 - core)
    own = spread_half(hi_ref, lo_ref, core)
    zero = jnp.zeros_like(own)
    is_key = core == 0
    send_k[...] = (sib_k[...] + jnp.where(is_key, other, zero)).astype(BF16)
    send_v[...] = (sib_v[...] + jnp.where(is_key, zero, other)).astype(BF16)
    total_k[...] = own_k[...] + jnp.where(is_key, own, zero)
    total_v[...] = own_v[...] + jnp.where(is_key, zero, own)


def context_grad_kernel(grad_ref, weight_ref, out_ref, acc_ref):
    step = pl.program_id(0)
    part = mm(grad_ref[0], weight_ref[...], ((1,), (1,)))

    @pl.when(step == 0)
    def _():
        acc_ref[...] = part

    @pl.when(step > 0)
    def _():
        acc_ref[...] += part

    @pl.when(step == pl.num_programs(0) - 1)
    def _():
        out_ref[...] = acc_ref[...].astype(BF16)


def weight_term_kernel(grad_ref, context_ref, out_ref):
    out_ref[...] = mm(grad_ref[0], context_ref[...], ((0,), (0,))).astype(BF16)


def context_grad_of(full_grad, out_weight):
    parts, rows, width = full_grad.shape
    features = out_weight.shape[0]
    return pl.pallas_call(
        context_grad_kernel,
        grid=(parts,),
        in_specs=[
            pl.BlockSpec((1, rows, width), lambda z: (z, 0, 0)),
            pl.BlockSpec((features, width), lambda z: (0, z)),
        ],
        out_specs=pl.BlockSpec((rows, features), lambda z: (0, 0)),
        out_shape=jax.ShapeDtypeStruct((rows, features), BF16),
        scratch_shapes=[pltpu.VMEM((rows, features), F32)],
        name="context_grad",
    )(full_grad, out_weight)


def weight_term_of(full_grad, context):
    parts, rows, width = full_grad.shape
    features = context.shape[1]
    return pl.pallas_call(
        weight_term_kernel,
        grid=(parts,),
        in_specs=[
            pl.BlockSpec((1, rows, width), lambda z: (z, 0, 0)),
            pl.BlockSpec((rows, features), lambda z: (0, 0)),
        ],
        out_specs=pl.BlockSpec((width, features), lambda z: (z, 0)),
        out_shape=jax.ShapeDtypeStruct((parts * width, features), BF16),
        name="weight_term",
    )(full_grad, context)


def column_weights(block_doc, my_block, leaf_rows, level_count):
    leaf_iota = jnp.arange(leaf_rows, dtype=jnp.int32)
    block_parts = [
        jnp.full((leaf_rows,), my_block, jnp.int32),
        jnp.full((leaf_rows,), my_block ^ 1, jnp.int32),
    ]
    weight_parts = [jnp.ones((2 * leaf_rows,), F32)]
    for level_num in range(1, level_count):
        group_first = (my_block >> level_num ^ 1) << level_num
        block_parts.append(group_first + leaf_iota // (leaf_rows >> level_num))
        weight_parts.append(jnp.full((leaf_rows,), 2.0**level_num, F32))
    col_block = jnp.concatenate(block_parts)
    col_weight = jnp.concatenate(weight_parts)
    block_ids = jnp.arange(block_doc.shape[1], dtype=jnp.int32)
    col_onehot = (block_ids[:, None] == col_block[None, :]).astype(jnp.int32)
    col_doc = jnp.sum(block_doc[0][:, None] * col_onehot, axis=0)
    own_doc = jnp.sum(block_doc[0] * (block_ids == my_block).astype(jnp.int32))
    return jnp.where(col_doc == own_doc, col_weight, 0.0)[None]


def local(queries, keys, values, out_weight, out_grad, block_doc):
    seq_count = lax.axis_size("seq")
    level_count = seq_count.bit_length() - 1
    n_up = level_count - 1
    my_block = lax.axis_index("seq")
    place = my_block.astype(jnp.int32)[None]
    _, rows, features = queries.shape
    heads = features // DH
    cols = (level_count + 1) * rows
    scaling = 1.0 / math.sqrt(DH)
    queries, keys, values = queries[0], keys[0], values[0]
    tall = (rows, features)

    other_keys = swapped(keys, 0)
    other_values = swapped(values, 0)
    full_grad = lax.all_gather(out_grad[0], "head")
    (chain,) = whole_call(
        pool_first_kernel, place, (keys, values, other_keys, other_values), [(tall, BF16)], name="pool_leaf"
    )
    mine, other = [], []
    for level_num in range(1, level_count):
        got = swapped(chain, level_num)
        mine.append(got)
        other.append(swapped(got, 0))
        if level_num + 1 < level_count:
            (chain,) = whole_call(
                functools.partial(pool_kernel, level_num), place, (chain, got), [(tall, BF16)], name="pool_group"
            )
    col_weight = column_weights(block_doc, my_block, rows, level_count)
    context_grad = context_grad_of(full_grad, out_weight)

    slab = pl.BlockSpec((rows, DH), lambda h: (0, h))
    col_slab = pl.BlockSpec((cols, DH), lambda h: (0, h))
    prob_slab = pl.BlockSpec((1, rows, cols), lambda h: (h, 0, 0))
    up_slab = pl.BlockSpec((n_up, rows, DH), lambda h: (0, 0, h))
    context, prob, kcols, vcols = pl.pallas_call(
        functools.partial(forward_kernel, scaling, n_up),
        grid=(heads,),
        in_specs=[SMEM, pl.BlockSpec((1, cols), lambda h: (0, 0))] + [slab] * (5 + 2 * n_up),
        out_specs=[slab, prob_slab, col_slab, col_slab],
        out_shape=[
            jax.ShapeDtypeStruct(tall, BF16),
            jax.ShapeDtypeStruct((heads, rows, cols), BF16),
            jax.ShapeDtypeStruct((cols, features), BF16),
            jax.ShapeDtypeStruct((cols, features), BF16),
        ],
        name="attention_forward",
    )(place, col_weight, queries, keys, other_keys, values, other_values, *mine, *other)

    weight_term = weight_term_of(full_grad, context)
    weight_grad = lax.psum_scatter(weight_term, "seq", scatter_dimension=0, tiled=True).T

    query_grad, own_k, own_v, sib_k, sib_v, keep, send_up = pl.pallas_call(
        functools.partial(backward_kernel, scaling, n_up),
        grid=(heads,),
        in_specs=[SMEM, slab, prob_slab, slab, slab, col_slab, col_slab],
        out_specs=[slab] * 5 + [up_slab, up_slab],
        out_shape=[jax.ShapeDtypeStruct(tall, BF16)]
        + [jax.ShapeDtypeStruct(tall, F32)] * 4
        + [
            jax.ShapeDtypeStruct((n_up,) + tall, F32),
            jax.ShapeDtypeStruct((n_up,) + tall, BF16),
        ],
        name="attention_backward",
    )(place, queries, prob, context, context_grad, kcols, vcols)

    recv_up = swapped(send_up, 0)
    top = n_up - 1
    back = swapped((keep[top] + recv_up[top].astype(F32)).astype(BF16), level_count - 1)
    held = jnp.zeros(tall, F32)
    halves = [pltpu.VMEM(tall, BF16), pltpu.VMEM(tall, BF16)]
    for level_num in range(level_count - 2, 0, -1):
        level_block = pl.BlockSpec((1,) + tall, functools.partial(lambda at, i: (at, 0, 0), level_num - 1))
        same = pl.BlockSpec(tall, lambda i: (0, 0))
        send, held = pl.pallas_call(
            functools.partial(climb_kernel, level_num),
            grid=(1,),
            in_specs=[SMEM, same, same, level_block, level_block],
            out_specs=[same, same],
            out_shape=[jax.ShapeDtypeStruct(tall, BF16), jax.ShapeDtypeStruct(tall, F32)],
            scratch_shapes=halves,
            name="hand_down",
        )(place, held, back, keep, recv_up)
        back = swapped(send, level_num)
    send_k, send_v, total_k, total_v = whole_call(
        leaf_kernel,
        place,
        (held, back, own_k, own_v, sib_k, sib_v),
        [(tall, BF16), (tall, BF16), (tall, F32), (tall, F32)],
        scratch=halves,
        name="hand_down_leaf",
    )
    key_grad = (total_k + swapped(send_k, 0).astype(F32)).astype(BF16)
    value_grad = (total_v + swapped(send_v, 0).astype(F32)).astype(BF16)
    return context[None], query_grad[None], key_grad[None], value_grad[None], weight_grad


def solution(mesh):
    placed = (
        P(None, "seq", "head"),
        P(None, "seq", "head"),
        P(None, "seq", "head"),
        P("head", None),
        P(None, "seq", "head"),
        P(),
    )
    return jax.shard_map(
        local,
        mesh=mesh,
        in_specs=placed,
        out_specs=(
            P(None, "seq", "head"),
            P(None, "seq", "head"),
            P(None, "seq", "head"),
            P(None, "seq", "head"),
            P("head", "seq"),
        ),
        check_vma=False,
    )
```

profile of v0, /device:TPU:1, one launch (start us, length us, event | category | flops | bytes accessed | tf_op | source)
XLA Modules:
  0.0 174.9 jit_solution(4046892189458552757)
XLA Ops:
  8.0 3.3 %collective-permute-start = (bf16[256,512]{1,0:T(8,128)(2,1)}, bf16[256,512]{1,0:T(8,128)(2,1)S(1)}, u32[]{:S(2)}, u32[]{:S(2)}) collective-permute-start(bf16[256,512]{1,0:T(8,128)(2,1)} %bitcast.18), channel_id=1, source_target_pairs={{0,8},{8,0},{16,24},{24,16},{32,40},{40,32},{48,56},{56,48},{64,72... | collective-permute-start | bytes 786440 | tf_op jit(solution)/shard_map/ppermute | solution.py:19
  13.7 2.1 %pool_leaf.1.mine_ref = bf16[256,512]{1,0:T(8,128)(2,1)} custom-call(s32[1]{0:T(128)} %bitcast.place_ref, bf16[256,512]{1,0:T(8,128)(2,1)} %bitcast.19, bf16[256,512]{1,0:T(8,128)(2,1)} %bitcast.22, bf16[256,512]{1,0:T(8,128)(2,1)} %copy-done.1, bf16[256,512]{1,0:T(8,128)(2,1)} %copy-done.2), custom_call_target="tpu_custom_call" | custom-call | tf_op jit(solution)/shard_map/pool_leaf/pallas_call | solution.py:70
  15.9 7.7 %collective-permute-done.2.other_ref.refs_4_ = bf16[256,512]{1,0:T(8,128)(2,1)S(1)} collective-permute-done((bf16[256,512]{1,0:T(8,128)(2,1)}, bf16[256,512]{1,0:T(8,128)(2,1)S(1)}, u32[]{:S(2)}, u32[]{:S(2)}) %collective-permute-start.2) | collective-permute-done | bytes 262176 | tf_op jit(solution)/shard_map/ppermute | solution.py:19
  24.3 2.0 %pool_group.3.mine_ref = bf16[256,512]{1,0:T(8,128)(2,1)} custom-call(s32[1]{0:T(128)} %bitcast.place_ref, bf16[256,512]{1,0:T(8,128)(2,1)} %pool_leaf.1.mine_ref, bf16[256,512]{1,0:T(8,128)(2,1)} %copy-done.3), custom_call_target="tpu_custom_call" | custom-call | tf_op jit(solution)/shard_map/pool_group/pallas_call | solution.py:70
  27.3 7.1 %collective-permute-done.3.other_ref.refs_5_ = bf16[256,512]{1,0:T(8,128)(2,1)S(1)} collective-permute-done((bf16[256,512]{1,0:T(8,128)(2,1)}, bf16[256,512]{1,0:T(8,128)(2,1)S(1)}, u32[]{:S(2)}, u32[]{:S(2)}) %collective-permute-start.3) | collective-permute-done | bytes 262176 | tf_op jit(solution)/shard_map/ppermute | solution.py:19
  37.1 6.0 %collective-permute-done.4.other_ref.refs_6_ = bf16[256,512]{1,0:T(8,128)(2,1)S(1)} collective-permute-done((bf16[256,512]{1,0:T(8,128)(2,1)}, bf16[256,512]{1,0:T(8,128)(2,1)S(1)}, u32[]{:S(2)}, u32[]{:S(2)}) %collective-permute-start.4) | collective-permute-done | bytes 262176 | tf_op jit(solution)/shard_map/ppermute | solution.py:19
  46.6 3.2 %collective-permute-start.6 = (bf16[256,512]{1,0:T(8,128)(2,1)}, bf16[256,512]{1,0:T(8,128)(2,1)S(1)}, u32[]{:S(2)}, u32[]{:S(2)}) collective-permute-start(bf16[256,512]{1,0:T(8,128)(2,1)} %copy-done.3), channel_id=1, source_target_pairs={{0,8},{8,0},{16,24},{24,16},{32,40},{40,32},{48,56},{56,48},{64,72... | collective-permute-start | bytes 786440 | tf_op jit(solution)/shard_map/ppermute | solution.py:19
  50.4 2.4 %collective-permute-done.5.refs_7_ = bf16[256,512]{1,0:T(8,128)(2,1)S(1)} collective-permute-done((bf16[256,512]{1,0:T(8,128)(2,1)}, bf16[256,512]{1,0:T(8,128)(2,1)S(1)}, u32[]{:S(2)}, u32[]{:S(2)}) %collective-permute-start.5) | collective-permute-done | bytes 262176 | tf_op jit(solution)/shard_map/ppermute | solution.py:19
  52.8 3.7 %collective-permute-start.9 = (bf16[256,512]{1,0:T(8,128)(2,1)S(1)}, bf16[256,512]{1,0:T(8,128)(2,1)S(1)}, u32[]{:S(2)}, u32[]{:S(2)}) collective-permute-start(bf16[256,512]{1,0:T(8,128)(2,1)S(1)} %collective-permute-done.5.refs_7_), channel_id=1, source_target_pairs={{0,8},{8,0},{16,24},{24,16},{32,40},{40,32},{48,56},{56,48},{64,72... | collective-permute-start | bytes 786440 | tf_op jit(solution)/shard_map/ppermute | solution.py:19
  59.3 7.1 %attention_forward.1 = (bf16[256,512]{1,0:T(8,128)(2,1)}, bf16[4,256,1536]{2,1,0:T(8,128)(2,1)}, bf16[1536,512]{1,0:T(8,128)(2,1)}, bf16[1536,512]{1,0:T(8,128)(2,1)}) custom-call(s32[1]{0:T(128)} %bitcast.place_ref, f32[1,1536]{1,0:T(1,128)} %select_n.33.weight_ref, bf16[256,512]{1,0:T(8,128)(2,1)} %bitcast.15, bf16[256,512]{1,0:T(8,128)(2,1)} %bitcast.20, ...), custom_call_target="tpu_custom_call" | custom-call | tf_op jit(solution)/shard_map/attention_forward/pallas_call | solution.py:293
  66.4 7.2 %weight_term.1 = bf16[4096,512]{1,0:T(8,128)(2,1)} custom-call(bf16[8,256,512]{2,1,0:T(8,128)(2,1)} %all-gather.2.cloned.1.call-done.grad_ref, bf16[256,512]{1,0:T(8,128)(2,1)} %get-tuple-element.26.context_ref), custom_call_target="tpu_custom_call" | custom-call | tf_op jit(solution)/shard_map/weight_term/pallas_call | solution.py:225
  73.7 7.3 %context_grad.1.grad_ref = bf16[256,512]{1,0:T(8,128)(2,1)} custom-call(bf16[8,256,512]{2,1,0:T(8,128)(2,1)} %all-gather.2.cloned.1.call-done.grad_ref, bf16[512,4096]{1,0:T(8,128)(2,1)} %weight_ref.1), custom_call_target="tpu_custom_call" | custom-call | tf_op jit(solution)/shard_map/context_grad/pallas_call | solution.py:208
  81.0 7.8 %attention_backward.1 = (bf16[256,512]{1,0:T(8,128)(2,1)}, f32[256,512]{1,0:T(8,128)}, f32[256,512]{1,0:T(8,128)}, f32[256,512]{1,0:T(8,128)}, f32[256,512]{1,0:...) custom-call(s32[1]{0:T(128)} %bitcast.place_ref, bf16[256,512]{1,0:T(8,128)(2,1)} %bitcast.16, ...), custom_call_target="tpu_custom_call" | custom-call | tf_op jit(solution)/shard_map/attention_backward/pallas_call | solution.py:310
  89.0 2.9 %collective-permute-done.10.recv_ref = bf16[4,256,512]{2,1,0:T(8,128)(2,1)S(1)} collective-permute-done((bf16[4,256,512]{2,1,0:T(8,128)(2,1)}, bf16[4,256,512]{2,1,0:T(8,128)(2,1)S(1)}, u32[]{:S(2)}, u32[]{:S(2)}) %collective-permute-start.10) | collective-permute-done | bytes 1048608 | tf_op jit(solution)/shard_map/ppermute | solution.py:19
  94.2 8.3 %collective-permute-done.11.back_ref = bf16[256,512]{1,0:T(8,128)(2,1)S(1)} collective-permute-done((bf16[256,512]{1,0:T(8,128)(2,1)S(1)}, bf16[256,512]{1,0:T(8,128)(2,1)S(1)}, u32[]{:S(2)}, u32[]{:S(2)}) %collective-permute-start.11) | collective-permute-done | bytes 262176 | tf_op jit(solution)/shard_map/ppermute | solution.py:19
  103.4 2.7 %hand_down.3 = (bf16[256,512]{1,0:T(8,128)(2,1)}, f32[256,512]{1,0:T(8,128)}) custom-call(s32[1]{0:T(128)} %bitcast.place_ref, f32[256,512]{1,0:T(8,128)} %broadcast_in_dim.37.held_ref, bf16[256,512]{1,0:T(8,128)(2,1)} %copy-done.13, f32[4,256,512]{2,1,0:T(8,128)} %get-tuple-element.31.keep_ref, bf16[4,256,512]{2,1,0:T(8,128)(2,1)} %copy-done), custom_call_target="tpu_custom_call" | custom-call | tf_op jit(solution)/shard_map/hand_down/pallas_call | solution.py:332
  106.1 7.1 %collective-permute-done.12.back_ref = bf16[256,512]{1,0:T(8,128)(2,1)S(1)} collective-permute-done((bf16[256,512]{1,0:T(8,128)(2,1)}, bf16[256,512]{1,0:T(8,128)(2,1)S(1)}, u32[]{:S(2)}, u32[]{:S(2)}) %collective-permute-start.12) | collective-permute-done | bytes 262176 | tf_op jit(solution)/shard_map/ppermute | solution.py:19
  113.9 2.7 %hand_down.4 = (bf16[256,512]{1,0:T(8,128)(2,1)}, f32[256,512]{1,0:T(8,128)}) custom-call(s32[1]{0:T(128)} %bitcast.place_ref, f32[256,512]{1,0:T(8,128)} %get-tuple-element.33.held_ref, bf16[256,512]{1,0:T(8,128)(2,1)} %copy-done.14, f32[4,256,512]{2,1,0:T(8,128)} %get-tuple-element.31.keep_ref, bf16[4,256,512]{2,1,0:T(8,128)(2,1)} %copy-done), custom_call_target="tpu_custom_call" | custom-call | tf_op jit(solution)/shard_map/hand_down/pallas_call | solution.py:332
  117.5 6.5 %collective-permute-done.13.back_ref = bf16[256,512]{1,0:T(8,128)(2,1)S(1)} collective-permute-done((bf16[256,512]{1,0:T(8,128)(2,1)}, bf16[256,512]{1,0:T(8,128)(2,1)S(1)}, u32[]{:S(2)}, u32[]{:S(2)}) %collective-permute-start.13) | collective-permute-done | bytes 262176 | tf_op jit(solution)/shard_map/ppermute | solution.py:19
  124.7 2.7 %hand_down.5 = (bf16[256,512]{1,0:T(8,128)(2,1)}, f32[256,512]{1,0:T(8,128)}) custom-call(s32[1]{0:T(128)} %bitcast.place_ref, f32[256,512]{1,0:T(8,128)} %get-tuple-element.35.held_ref, bf16[256,512]{1,0:T(8,128)(2,1)} %copy-done.12, f32[4,256,512]{2,1,0:T(8,128)} %get-tuple-element.31.keep_ref, bf16[4,256,512]{2,1,0:T(8,128)(2,1)} %copy-done), custom_call_target="tpu_custom_call" | custom-call | tf_op jit(solution)/shard_map/hand_down/pallas_call | solution.py:332
  127.4 10.8 %collective-permute-done.14.back_ref = bf16[256,512]{1,0:T(8,128)(2,1)S(1)} collective-permute-done((bf16[256,512]{1,0:T(8,128)(2,1)}, bf16[256,512]{1,0:T(8,128)(2,1)S(1)}, u32[]{:S(2)}, u32[]{:S(2)}) %collective-permute-start.14) | collective-permute-done | bytes 262176 | tf_op jit(solution)/shard_map/ppermute | solution.py:19
  138.9 3.4 %hand_down_leaf.1 = (bf16[256,512]{1,0:T(8,128)(2,1)}, bf16[256,512]{1,0:T(8,128)(2,1)}, f32[256,512]{1,0:T(8,128)}, f32[256,512]{1,0:T(8,128)}) custom-call(s32[1]{0:T(128)} %bitcast.place_ref, f32[256,512]{1,0:T(8,128)} %get-tuple-element.37.held_ref, bf16[256,512]{1,0:T(8,128)(2,1)} %copy-done.11, f32[256,512]{1,0:T(8,128)} %get-tuple-element.39.own_k, ...), custom_call_target="tpu_custom_call" | custom-call | tf_op jit(solution)/shard_map/hand_down_leaf/pallas_call | solution.py:70
  142.2 4.9 %collective-permute-start.16 = (bf16[256,512]{1,0:T(8,128)(2,1)}, bf16[256,512]{1,0:T(8,128)(2,1)S(1)}, u32[]{:S(2)}, u32[]{:S(2)}) collective-permute-start(bf16[256,512]{1,0:T(8,128)(2,1)} %get-tuple-element.46), channel_id=1, source_target_pairs={{0,8},{8,0},{16,24},{24,16},{32,40},{40,32},{48,56},{56,48},{64,72... | collective-permute-start | bytes 786440 | tf_op jit(solution)/shard_map/ppermute | solution.py:19
  152.2 14.2 %reduce-scatter.2.cloned.1.call-done = bf16[128,512]{1,0:T(8,128)(2,1)} async-done(((bf16[4096,512]{1,0:T(8,128)(2,1)}), bf16[128,512]{1,0:T(8,128)(2,1)}) %reduce-scatter.2.cloned.1.call-update) | async-done | bytes 131088 | tf_op jit(solution)/shard_map/reduce_scatter | solution.py:308
  (78 shorter events, 27.4 us)
Async XLA Ops:
  7.2 49.9 %copy-start.15 = (f32[1536]{0:T(1024)S(1)}, f32[1536]{0:T(1024)}, u32[]{:S(2)}) copy-start(f32[1536]{0:T(1024)} %constant.83.clone.1) | copy-start | bytes 18436
  7.2 39.4 %copy-start.16 = (s32[1,32]{1,0:T(1,128)S(1)}, s32[1,32]{1,0:T(1,128)}, u32[]{:S(2)}) copy-start(s32[1,32]{1,0:T(1,128)} %param.11) | copy-start | bytes 388
  7.2 59.2 %all-gather.2.cloned.1.call-start = ((), (), s32[]{:S(2)}) async-start(), calls=%async_computation.1 | async-start | bytes 2359296 | tf_op jit(solution)/shard_map/all_gather | solution.py:273
  7.9 158.5 %reduce-scatter.2.cloned.1.call-start = ((), (), s32[]{:S(2)}) async-start(), calls=%async_computation.2 | async-start | bytes 4325376 | tf_op jit(solution)/shard_map/reduce_scatter | solution.py:308
  8.0 4.7 %collective-permute-start = (bf16[256,512]{1,0:T(8,128)(2,1)}, bf16[256,512]{1,0:T(8,128)(2,1)S(1)}, u32[]{:S(2)}, u32[]{:S(2)}) collective-permute-start(bf16[256,512]{1,0:T(8,128)(2,1)} %bitcast.18), channel_id=1, source_target_pairs={{0,8},{8,0},{16,24},{24,16},{32,40},{40,32},{48,56},{56,48},{64,72... | collective-permute-start | bytes 786440 | tf_op jit(solution)/shard_map/ppermute | solution.py:19
  11.3 1.7 collective-permute-start.1
  15.9 7.7 %collective-permute-start.2 = (bf16[256,512]{1,0:T(8,128)(2,1)}, bf16[256,512]{1,0:T(8,128)(2,1)S(1)}, u32[]{:S(2)}, u32[]{:S(2)}) collective-permute-start(bf16[256,512]{1,0:T(8,128)(2,1)} %pool_leaf.1.mine_ref), channel_id=1, source_target_pairs={{0,16},{8,24},{16,0},{24,8},{32,48},{40,56},{48,32},{56,40},{64,80... | collective-permute-start | bytes 786440 | tf_op jit(solution)/shard_map/ppermute | solution.py:19
  26.3 8.1 %collective-permute-start.3 = (bf16[256,512]{1,0:T(8,128)(2,1)}, bf16[256,512]{1,0:T(8,128)(2,1)S(1)}, u32[]{:S(2)}, u32[]{:S(2)}) collective-permute-start(bf16[256,512]{1,0:T(8,128)(2,1)} %pool_group.3.mine_ref), channel_id=1, source_target_pairs={{0,48},{8,56},{16,32},{24,40},{32,16},{40,24},{48,0},{56,8},{64,11... | collective-permute-start | bytes 786440 | tf_op jit(solution)/shard_map/ppermute | solution.py:19
  37.0 6.0 %collective-permute-start.4 = (bf16[256,512]{1,0:T(8,128)(2,1)}, bf16[256,512]{1,0:T(8,128)(2,1)S(1)}, u32[]{:S(2)}, u32[]{:S(2)}) collective-permute-start(bf16[256,512]{1,0:T(8,128)(2,1)} %pool_group.4.mine_ref), channel_id=1, source_target_pairs={{0,64},{8,72},{16,80},{24,88},{32,96},{40,104},{48,112},{56,120},{... | collective-permute-start | bytes 786440 | tf_op jit(solution)/shard_map/ppermute | solution.py:19
  45.7 7.0 %collective-permute-start.5 = (bf16[256,512]{1,0:T(8,128)(2,1)}, bf16[256,512]{1,0:T(8,128)(2,1)S(1)}, u32[]{:S(2)}, u32[]{:S(2)}) collective-permute-start(bf16[256,512]{1,0:T(8,128)(2,1)} %pool_group.5), channel_id=1, source_target_pairs={{0,192},{8,200},{16,208},{24,216},{32,224},{40,232},{48,240},{56,2... | collective-permute-start | bytes 786440 | tf_op jit(solution)/shard_map/ppermute | solution.py:19
  46.6 11.7 %collective-permute-start.6 = (bf16[256,512]{1,0:T(8,128)(2,1)}, bf16[256,512]{1,0:T(8,128)(2,1)S(1)}, u32[]{:S(2)}, u32[]{:S(2)}) collective-permute-start(bf16[256,512]{1,0:T(8,128)(2,1)} %copy-done.3), channel_id=1, source_target_pairs={{0,8},{8,0},{16,24},{24,16},{32,40},{40,32},{48,56},{56,48},{64,72... | collective-permute-start | bytes 786440 | tf_op jit(solution)/shard_map/ppermute | solution.py:19
  49.9 8.4 %collective-permute-start.7 = (bf16[256,512]{1,0:T(8,128)(2,1)}, bf16[256,512]{1,0:T(8,128)(2,1)S(1)}, u32[]{:S(2)}, u32[]{:S(2)}) collective-permute-start(bf16[256,512]{1,0:T(8,128)(2,1)} %copy-done.4), channel_id=1, source_target_pairs={{0,8},{8,0},{16,24},{24,16},{32,40},{40,32},{48,56},{56,48},{64,72... | collective-permute-start | bytes 786440 | tf_op jit(solution)/shard_map/ppermute | solution.py:19
  50.0 8.3 %collective-permute-start.8 = (bf16[256,512]{1,0:T(8,128)(2,1)}, bf16[256,512]{1,0:T(8,128)(2,1)S(1)}, u32[]{:S(2)}, u32[]{:S(2)}) collective-permute-start(bf16[256,512]{1,0:T(8,128)(2,1)} %copy-done.5), channel_id=1, source_target_pairs={{0,8},{8,0},{16,24},{24,16},{32,40},{40,32},{48,56},{56,48},{64,72... | collective-permute-start | bytes 786440 | tf_op jit(solution)/shard_map/ppermute | solution.py:19
  52.8 5.6 %copy-start.6 = (bf16[256,512]{1,0:T(8,128)(2,1)}, bf16[256,512]{1,0:T(8,128)(2,1)S(1)}, u32[]{:S(2)}) copy-start(bf16[256,512]{1,0:T(8,128)(2,1)S(1)} %collective-permute-done.5.refs_7_) | copy-start | bytes 786436
  52.8 5.6 %collective-permute-start.9 = (bf16[256,512]{1,0:T(8,128)(2,1)S(1)}, bf16[256,512]{1,0:T(8,128)(2,1)S(1)}, u32[]{:S(2)}, u32[]{:S(2)}) collective-permute-start(bf16[256,512]{1,0:T(8,128)(2,1)S(1)} %collective-permute-done.5.refs_7_), channel_id=1, source_target_pairs={{0,8},{8,0},{16,24},{24,16},{32,40},{40,32},{48,56},{56,48},{64,72... | collective-permute-start | bytes 786440 | tf_op jit(solution)/shard_map/ppermute | solution.py:19
  58.4 0.9 copy-start.10
  88.9 3.0 %collective-permute-start.10 = (bf16[4,256,512]{2,1,0:T(8,128)(2,1)}, bf16[4,256,512]{2,1,0:T(8,128)(2,1)S(1)}, u32[]{:S(2)}, u32[]{:S(2)}) collective-permute-start(bf16[4,256,512]{2,1,0:T(8,128)(2,1)} %get-tuple-element.32), channel_id=1, source_target_pairs={{0,8},{8,0},{16,24},{24,16},{32,40},{40,32},{48,56},{56,48},{64,72... | collective-permute-start | bytes 3145736 | tf_op jit(solution)/shard_map/ppermute | solution.py:19
  91.9 11.5 %copy-start = (bf16[4,256,512]{2,1,0:T(8,128)(2,1)}, bf16[4,256,512]{2,1,0:T(8,128)(2,1)S(1)}, u32[]{:S(2)}) copy-start(bf16[4,256,512]{2,1,0:T(8,128)(2,1)S(1)} %collective-permute-done.10.recv_ref) | copy-start | bytes 3145732
  93.4 9.1 %collective-permute-start.11 = (bf16[256,512]{1,0:T(8,128)(2,1)S(1)}, bf16[256,512]{1,0:T(8,128)(2,1)S(1)}, u32[]{:S(2)}, u32[]{:S(2)}) collective-permute-start(bf16[256,512]{1,0:T(8,128)(2,1)S(1)} %fusion), channel_id=1, source_target_pairs={{0,192},{8,200},{16,208},{24,216},{32,224},{40,232},{48,240},{56,2... | collective-permute-start | bytes 786440 | tf_op jit(solution)/shard_map/ppermute | solution.py:19
  106.1 7.1 %collective-permute-start.12 = (bf16[256,512]{1,0:T(8,128)(2,1)}, bf16[256,512]{1,0:T(8,128)(2,1)S(1)}, u32[]{:S(2)}, u32[]{:S(2)}) collective-permute-start(bf16[256,512]{1,0:T(8,128)(2,1)} %get-tuple-element.34), channel_id=1, source_target_pairs={{0,64},{8,72},{16,80},{24,88},{32,96},{40,104},{48,112},{56,120},{... | collective-permute-start | bytes 786440 | tf_op jit(solution)/shard_map/ppermute | solution.py:19
  116.6 7.4 %collective-permute-start.13 = (bf16[256,512]{1,0:T(8,128)(2,1)}, bf16[256,512]{1,0:T(8,128)(2,1)S(1)}, u32[]{:S(2)}, u32[]{:S(2)}) collective-permute-start(bf16[256,512]{1,0:T(8,128)(2,1)} %get-tuple-element.36), channel_id=1, source_target_pairs={{0,48},{8,56},{16,32},{24,40},{32,16},{40,24},{48,0},{56,8},{64,11... | collective-permute-start | bytes 786440 | tf_op jit(solution)/shard_map/ppermute | solution.py:19
  127.4 10.8 %collective-permute-start.14 = (bf16[256,512]{1,0:T(8,128)(2,1)}, bf16[256,512]{1,0:T(8,128)(2,1)S(1)}, u32[]{:S(2)}, u32[]{:S(2)}) collective-permute-start(bf16[256,512]{1,0:T(8,128)(2,1)} %get-tuple-element.38), channel_id=1, source_target_pairs={{0,16},{8,24},{16,0},{24,8},{32,48},{40,56},{48,32},{56,40},{64,80... | collective-permute-start | bytes 786440 | tf_op jit(solution)/shard_map/ppermute | solution.py:19
  142.2 6.3 %collective-permute-start.16 = (bf16[256,512]{1,0:T(8,128)(2,1)}, bf16[256,512]{1,0:T(8,128)(2,1)S(1)}, u32[]{:S(2)}, u32[]{:S(2)}) collective-permute-start(bf16[256,512]{1,0:T(8,128)(2,1)} %get-tuple-element.46), channel_id=1, source_target_pairs={{0,8},{8,0},{16,24},{24,16},{32,40},{40,32},{48,56},{56,48},{64,72... | collective-permute-start | bytes 786440 | tf_op jit(solution)/shard_map/ppermute | solution.py:19
  147.2 3.2 %collective-permute-start.15 = (bf16[256,512]{1,0:T(8,128)(2,1)}, bf16[256,512]{1,0:T(8,128)(2,1)S(1)}, u32[]{:S(2)}, u32[]{:S(2)}) collective-permute-start(bf16[256,512]{1,0:T(8,128)(2,1)} %get-tuple-element.44), channel_id=1, source_target_pairs={{0,8},{8,0},{16,24},{24,16},{32,40},{40,32},{48,56},{56,48},{64,72... | collective-permute-start | bytes 786440 | tf_op jit(solution)/shard_map/ppermute | solution.py:19
  (12 other events, 8.9 us)
Sparse Core Ops, SparseCore 0:
  9.8 41.1 all-gather.1
  73.8 92.5 reduce-scatter.1
where the time goes:
time: 176 us; the launch traced here: 175 us
  waiting for transfers between devices  76.7 us (44%)
  Pallas kernels  49.1 us (28%)
  starting transfers between devices  19.4 us (11%)
  between operations  14.2 us (8%)
  local copies, waits for them, and re-layouts  8.99 us (5%)
  other arithmetic  6.56 us (4%)
    ppermute x17, waiting for transfers between devices, swapped(): lax.ppermute(value, 'seq', [(i, i ^ HOPS[level_num]) for i in range(count)])  61.7 us
    ppermute x17, starting transfers between devices, swapped(): lax.ppermute(value, 'seq', [(i, i ^ HOPS[level_num]) for i in range(count)])  19.3 us
    reduce_scatter x1, waiting for transfers between devices, local(): lax.psum_scatter(weight_term, 'seq', scatter_dimension=0, tiled=True)  14.2 us
    pallas_call x5, Pallas kernels, whole_call(): pl.pallas_call(kernel, in_specs=[SMEM] + [VMEM] * len(args), out_specs=[V...  11.4 us
    pallas_call x3, Pallas kernels, local(): pl.pallas_call(functools.partial(climb_kernel, level_num), grid=(1,), in_...  8.14 us
    pallas_call x1, Pallas kernels, local(): pl.pallas_call(functools.partial(backward_kernel, scaling, n_up), grid=(h...  7.84 us
    unnamed x37, local copies, waits for them, and re-layouts  7.51 us
    pallas_call x1, Pallas kernels, context_grad_of(): pl.pallas_call(context_grad_kernel, grid=(parts,), in_specs=[pl.BlockSpec...  7.33 us
  transfers between devices with their start and end apart: 19, of which 13 were waited for; matrix products, arithmetic and copies ran while one was open for 5% of the time, Pallas kernels for 24%

commit v1 on v0

--- a/solution.py
+++ b/solution.py
@@ -50,31 +50,32 @@
     pool_into(out_ref, bit, mine_ref[...], other_ref[...])
 
 
-def pool_first_kernel(place_ref, key_ref, value_ref, other_key_ref, other_value_ref, out_ref):
+def pool_first_kernel(place_ref, mine_k, mine_v, other_k, other_v, *out_refs):
     core = place_ref[0] & 1
 
-    @pl.when(core == 0)
-    def _():
-        pool_into(out_ref, core, key_ref[...], other_key_ref[...])
-
-    @pl.when(core == 1)
-    def _():
-        pool_into(out_ref, core, value_ref[...], other_value_ref[...])
+    def pooled(mine_ref, other_ref):
+        width = mine_ref.shape[1] // len(out_refs)
+        for i, out_ref in enumerate(out_refs):
+            part = slice(i * width, (i + 1) * width)
+            pool_into(out_ref, core, mine_ref[:, part], other_ref[:, part])
+
+    pl.when(core == 0)(lambda: pooled(mine_k, other_k))
+    pl.when(core == 1)(lambda: pooled(mine_v, other_v))
 
 
 SMEM = pl.BlockSpec(memory_space=pltpu.SMEM)
 VMEM = pl.BlockSpec(memory_space=pltpu.VMEM)
 
 
-def whole_call(kernel, place, args, outs, scratch=(), name=None):
+def near_call(kernel, place, args, outs, scratch=(), name=None):
     return pl.pallas_call(
         kernel,
         in_specs=[SMEM] + [VMEM] * len(args),
         out_specs=[VMEM] * len(outs),
-        out_shape=[jax.ShapeDtypeStruct(s, d) for s, d in outs],
+        out_shape=[pltpu.VMEM(s, d) for s, d in outs],
         scratch_shapes=list(scratch),
         name=name,
-    )(place, *args)
+    )(place, *[pltpu.with_memory_space_constraint(a, pltpu.VMEM) for a in args])
 
 
 def gather_columns(core, dest_k, dest_v, firsts, mine, other):
@@ -157,11 +158,20 @@
     lo_ref[...] = (held - hi.astype(F32)).astype(BF16)
 
 
-def climb_kernel(level_num, place_ref, held_ref, back_ref, keep_ref, recv_ref, send_ref, own_ref, hi_ref, lo_ref):
+def top_kernel(at, place_ref, keep_ref, recv_ref, send_ref):
+    send_ref[...] = (keep_ref[at] + recv_ref[at].astype(F32)).astype(BF16)
+
+
+def climb_kernel(level_num, place_ref, keep_ref, recv_ref, back_ref, *refs):
+    held_ref = refs[0] if len(refs) == 5 else None
+    send_ref, own_ref, hi_ref, lo_ref = refs[-4:]
     bit = (place_ref[0] >> level_num) & 1
-    split_held(hi_ref, lo_ref, held_ref[...] + back_ref[...].astype(F32))
+    held = back_ref[...].astype(F32)
+    if held_ref is not None:
+        held = held + held_ref[...]
+    split_held(hi_ref, lo_ref, held)
     other = spread_half(hi_ref, lo_ref, 1 - bit)
-    send_ref[...] = (keep_ref[0] + recv_ref[0].astype(F32) + other).astype(BF16)
+    send_ref[...] = (keep_ref[level_num - 1] + recv_ref[level_num - 1].astype(F32) + other).astype(BF16)
     own_ref[...] = spread_half(hi_ref, lo_ref, bit)
 
 
@@ -181,58 +191,39 @@
     total_v[...] = own_v[...] + jnp.where(is_key, zero, own)
 
 
-def context_grad_kernel(grad_ref, weight_ref, out_ref, acc_ref):
-    step = pl.program_id(0)
-    part = mm(grad_ref[0], weight_ref[...], ((1,), (1,)))
-
-    @pl.when(step == 0)
-    def _():
-        acc_ref[...] = part
-
-    @pl.when(step > 0)
-    def _():
-        acc_ref[...] += part
-
-    @pl.when(step == pl.num_programs(0) - 1)
-    def _():
-        out_ref[...] = acc_ref[...].astype(BF16)
-
-
-def weight_term_kernel(grad_ref, context_ref, out_ref):
-    out_ref[...] = mm(grad_ref[0], context_ref[...], ((0,), (0,))).astype(BF16)
-
-
-def context_grad_of(full_grad, out_weight):
-    parts, rows, width = full_grad.shape
-    features = out_weight.shape[0]
-    return pl.pallas_call(
-        context_grad_kernel,
-        grid=(parts,),
-        in_specs=[
-            pl.BlockSpec((1, rows, width), lambda z: (z, 0, 0)),
-            pl.BlockSpec((features, width), lambda z: (0, z)),
-        ],
-        out_specs=pl.BlockSpec((rows, features), lambda z: (0, 0)),
-        out_shape=jax.ShapeDtypeStruct((rows, features), BF16),
-        scratch_shapes=[pltpu.VMEM((rows, features), F32)],
-        name="context_grad",
-    )(full_grad, out_weight)
-
-
-def weight_term_of(full_grad, context):
-    parts, rows, width = full_grad.shape
-    features = context.shape[1]
-    return pl.pallas_call(
-        weight_term_kernel,
-        grid=(parts,),
-        in_specs=[
-            pl.BlockSpec((1, rows, width), lambda z: (z, 0, 0)),
-            pl.BlockSpec((rows, features), lambda z: (0, 0)),
-        ],
-        out_specs=pl.BlockSpec((width, features), lambda z: (z, 0)),
-        out_shape=jax.ShapeDtypeStruct((parts * width, features), BF16),
-        name="weight_term",
-    )(full_grad, context)
+def context_grad_kernel(offsets, place_ref, weight_ref, *refs):
+    count = len(offsets)
+    grads, out_ref, send_ref = refs[:count], refs[count], refs[count + 1]
+    core = place_ref[0] & 1
+    total = None
+    for i, offset in enumerate(offsets):
+        at = (place_ref[1] + offset) % count
+        width = grads[i].shape[1]
+        part = mm(grads[i][...], weight_ref[:, pl.ds(pl.multiple_of(at * width, width), width)], ((1,), (1,)))
+        total = part if total is None else total + part
+        for j in range(2):
+            cols = pl.ds(pl.multiple_of((2 * j + 1 - core) * DH, DH), DH)
+            send_ref[i, :, j * DH : (j + 1) * DH] = grads[i][:, cols]
+    out_ref[...] = total.astype(BF16)
+
+
+def weight_term_kernel(offsets, n_parts, place_ref, *refs):
+    count = len(offsets)
+    grads, other_grads = refs[:count], refs[count]
+    mine, other = refs[count + 1 : count + 1 + n_parts], refs[count + 1 + n_parts : count + 1 + 2 * n_parts]
+    out_ref, turned_ref = refs[-2:]
+    core = place_ref[0] & 1
+    rows, width = mine[0].shape
+    for i in range(n_parts):
+        turned_ref[i * width : (i + 1) * width, :rows] = mine[i][...].astype(F32).T.astype(BF16)
+        turned_ref[i * width : (i + 1) * width, rows:] = other[i][...].astype(F32).T.astype(BF16)
+    for i, offset in enumerate(offsets):
+        at = (place_ref[1] + offset) % count
+        own = [grads[i][:, pl.ds(pl.multiple_of((2 * j + core) * DH, DH), DH)] for j in range(2)]
+        own = jnp.concatenate(own, axis=1)
+        term = mm(turned_ref[:, :rows], own, ((1,), (0,))) + mm(turned_ref[:, rows:], other_grads[i], ((1,), (0,)))
+        for j in range(2):
+            out_ref[2 * at + j] = term[:, j * DH : (j + 1) * DH].astype(BF16)
 
 
 def column_weights(block_doc, my_block, leaf_rows, level_count):
@@ -255,101 +246,172 @@
     return jnp.where(col_doc == own_doc, col_weight, 0.0)[None]
 
 
+def ring_gather(block, axis):
+    count = lax.axis_size(axis)
+    up = [(i, (i + 1) % count) for i in range(count)]
+    down = [(i, (i - 1) % count) for i in range(count)]
+    blocks = [(0, block)]
+    from_below, from_above = block, block
+    for step in range(1, count // 2 + 1):
+        from_below = lax.ppermute(from_below, axis, up)
+        blocks.append((-step % count, from_below))
+        if step < count - step:
+            from_above = lax.ppermute(from_above, axis, down)
+            blocks.append((step, from_above))
+    return blocks
+
+
+N_PARTS = 2
+
+
 def local(queries, keys, values, out_weight, out_grad, block_doc):
     seq_count = lax.axis_size("seq")
     level_count = seq_count.bit_length() - 1
     n_up = level_count - 1
     my_block = lax.axis_index("seq")
-    place = my_block.astype(jnp.int32)[None]
+    place = jnp.stack([my_block, lax.axis_index("head")]).astype(jnp.int32)
     _, rows, features = queries.shape
     heads = features // DH
+    part_heads = heads // N_PARTS
+    part_width = part_heads * DH
     cols = (level_count + 1) * rows
     scaling = 1.0 / math.sqrt(DH)
     queries, keys, values = queries[0], keys[0], values[0]
-    tall = (rows, features)
+    tall = (rows, part_width)
 
     other_keys = swapped(keys, 0)
     other_values = swapped(values, 0)
-    full_grad = lax.all_gather(out_grad[0], "head")
-    (chain,) = whole_call(
-        pool_first_kernel, place, (keys, values, other_keys, other_values), [(tall, BF16)], name="pool_leaf"
+    blocks = ring_gather(out_grad[0], "head")
+    offsets = tuple(o for o, _ in blocks)
+    full_grad = [b for _, b in blocks]
+    chains = near_call(
+        pool_first_kernel, place, (keys, values, other_keys, other_values), [(tall, BF16)] * N_PARTS, name="pool_leaf"
     )
-    mine, other = [], []
+    chains = list(chains)
+    mine, other = [[] for _ in chains], [[] for _ in chains]
     for level_num in range(1, level_count):
-        got = swapped(chain, level_num)
-        mine.append(got)
-        other.append(swapped(got, 0))
-        if level_num + 1 < level_count:
-            (chain,) = whole_call(
-                functools.partial(pool_kernel, level_num), place, (chain, got), [(tall, BF16)], name="pool_group"
-            )
+        for i in range(N_PARTS):
+            got = swapped(chains[i], level_num)
+            mine[i].append(got)
+            other[i].append(swapped(got, 0))
+            if level_num + 1 < level_count:
+                (chains[i],) = near_call(
+                    functools.partial(pool_kernel, level_num), place, (chains[i], got), [(tall, BF16)], name="pool_group"
+                )
     col_weight = column_weights(block_doc, my_block, rows, level_count)
-    context_grad = context_grad_of(full_grad, out_weight)
+    context_grad, send_grad = pl.pallas_call(
+        functools.partial(context_grad_kernel, offsets),
+        in_specs=[SMEM] + [VMEM] * (1 + len(offsets)),
+        out_specs=[VMEM, VMEM],
+        out_shape=[
+            jax.ShapeDtypeStruct((rows, features), BF16),
+            jax.ShapeDtypeStruct((len(offsets), rows, features // 2), BF16),
+        ],
+        name="context_grad",
+    )(place, out_weight, *full_grad)
+    other_grad = swapped(send_grad, 0)
 
     slab = pl.BlockSpec((rows, DH), lambda h: (0, h))
     col_slab = pl.BlockSpec((cols, DH), lambda h: (0, h))
     prob_slab = pl.BlockSpec((1, rows, cols), lambda h: (h, 0, 0))
     up_slab = pl.BlockSpec((n_up, rows, DH), lambda h: (0, 0, h))
-    context, prob, kcols, vcols = pl.pallas_call(
-        functools.partial(forward_kernel, scaling, n_up),
-        grid=(heads,),
-        in_specs=[SMEM, pl.BlockSpec((1, cols), lambda h: (0, 0))] + [slab] * (5 + 2 * n_up),
-        out_specs=[slab, prob_slab, col_slab, col_slab],
-        out_shape=[
-            jax.ShapeDtypeStruct(tall, BF16),
-            jax.ShapeDtypeStruct((heads, rows, cols), BF16),
-            jax.ShapeDtypeStruct((cols, features), BF16),
-            jax.ShapeDtypeStruct((cols, features), BF16),
-        ],
-        name="attention_forward",
-    )(place, col_weight, queries, keys, other_keys, values, other_values, *mine, *other)
-
-    weight_term = weight_term_of(full_grad, context)
-    weight_grad = lax.psum_scatter(weight_term, "seq", scatter_dimension=0, tiled=True).T
-
-    query_grad, own_k, own_v, sib_k, sib_v, keep, send_up = pl.pallas_call(
-        functools.partial(backward_kernel, scaling, n_up),
-        grid=(heads,),
-        in_specs=[SMEM, slab, prob_slab, slab, slab, col_slab, col_slab],
-        out_specs=[slab] * 5 + [up_slab, up_slab],
-        out_shape=[jax.ShapeDtypeStruct(tall, BF16)]
-        + [jax.ShapeDtypeStruct(tall, F32)] * 4
-        + [
-            jax.ShapeDtypeStruct((n_up,) + tall, F32),
-            jax.ShapeDtypeStruct((n_up,) + tall, BF16),
-        ],
-        name="attention_backward",
-    )(place, queries, prob, context, context_grad, kcols, vcols)
-
-    recv_up = swapped(send_up, 0)
-    top = n_up - 1
-    back = swapped((keep[top] + recv_up[top].astype(F32)).astype(BF16), level_count - 1)
-    held = jnp.zeros(tall, F32)
+    whole_slabs = [
+        pl.BlockSpec((rows, DH), functools.partial(lambda first, h: (0, first + h), i * part_heads))
+        for i in range(N_PARTS)
+    ]
+    forward = []
+    for i in range(N_PARTS):
+        forward.append(
+            pl.pallas_call(
+                functools.partial(forward_kernel, scaling, n_up),
+                grid=(part_heads,),
+                in_specs=[SMEM, pl.BlockSpec((1, cols), lambda h: (0, 0))]
+                + [whole_slabs[i]] * 5
+                + [slab] * (2 * n_up),
+                out_specs=[slab, prob_slab, col_slab, col_slab],
+                out_shape=[
+                    jax.ShapeDtypeStruct(tall, BF16),
+                    jax.ShapeDtypeStruct((part_heads, rows, cols), BF16),
+                    jax.ShapeDtypeStruct((cols, part_width), BF16),
+                    jax.ShapeDtypeStruct((cols, part_width), BF16),
+                ],
+                name="attention_forward",
+            )(place, col_weight, queries, keys, other_keys, values, other_values, *mine[i], *other[i])
+        )
+    contexts = [f[0] for f in forward]
+    other_contexts = [swapped(c, 0) for c in contexts]
+
+    weight_term = pl.pallas_call(
+        functools.partial(weight_term_kernel, offsets, N_PARTS),
+        in_specs=[SMEM] + [VMEM] * (len(offsets) + 1 + 2 * N_PARTS),
+        out_specs=VMEM,
+        out_shape=jax.ShapeDtypeStruct((seq_count // 2, features, DH), BF16),
+        scratch_shapes=[pltpu.VMEM((features, 2 * rows), BF16)],
+        name="weight_term",
+    )(place, *full_grad, other_grad, *contexts, *other_contexts)
+    weight_grad = scatter_sum(weight_term, seq_count)
+
+    partial_grads = []
+    for i in range(N_PARTS):
+        context, prob, kcols, vcols = forward[i]
+        partial_grads.append(
+            pl.pallas_call(
+                functools.partial(backward_kernel, scaling, n_up),
+                grid=(part_heads,),
+                in_specs=[SMEM, whole_slabs[i], prob_slab, slab, whole_slabs[i], col_slab, col_slab],
+                out_specs=[slab] * 5 + [up_slab, up_slab],
+                out_shape=[jax.ShapeDtypeStruct(tall, BF16)]
+                + [jax.ShapeDtypeStruct(tall, F32)] * 4
+                + [
+                    jax.ShapeDtypeStruct((n_up,) + tall, F32),
+                    jax.ShapeDtypeStruct((n_up,) + tall, BF16),
+                ],
+                name="attention_backward",
+            )(place, queries, prob, context, context_grad, kcols, vcols)
+        )
+    query_grad = jnp.concatenate([g[0] for g in partial_grads], axis=1)
     halves = [pltpu.VMEM(tall, BF16), pltpu.VMEM(tall, BF16)]
+    keep = [g[5] for g in partial_grads]
+    recv_up = [swapped(g[6], 0) for g in partial_grads]
+    back, held = [None] * N_PARTS, [None] * N_PARTS
+    for i in range(N_PARTS):
+        (send,) = near_call(
+            functools.partial(top_kernel, n_up - 1), place, (keep[i], recv_up[i]), [(tall, BF16)], name="hand_down_top"
+        )
+        back[i] = swapped(send, level_count - 1)
     for level_num in range(level_count - 2, 0, -1):
-        level_block = pl.BlockSpec((1,) + tall, functools.partial(lambda at, i: (at, 0, 0), level_num - 1))
-        same = pl.BlockSpec(tall, lambda i: (0, 0))
-        send, held = pl.pallas_call(
-            functools.partial(climb_kernel, level_num),
-            grid=(1,),
-            in_specs=[SMEM, same, same, level_block, level_block],
-            out_specs=[same, same],
-            out_shape=[jax.ShapeDtypeStruct(tall, BF16), jax.ShapeDtypeStruct(tall, F32)],
-            scratch_shapes=halves,
-            name="hand_down",
-        )(place, held, back, keep, recv_up)
-        back = swapped(send, level_num)
-    send_k, send_v, total_k, total_v = whole_call(
-        leaf_kernel,
-        place,
-        (held, back, own_k, own_v, sib_k, sib_v),
-        [(tall, BF16), (tall, BF16), (tall, F32), (tall, F32)],
-        scratch=halves,
-        name="hand_down_leaf",
-    )
-    key_grad = (total_k + swapped(send_k, 0).astype(F32)).astype(BF16)
-    value_grad = (total_v + swapped(send_v, 0).astype(F32)).astype(BF16)
+        for i in range(N_PARTS):
+            args = (keep[i], recv_up[i], back[i]) + (() if held[i] is None else (held[i],))
+            send, held[i] = near_call(
+                functools.partial(climb_kernel, level_num),
+                place,
+                args,
+                [(tall, BF16), (tall, F32)],
+                scratch=halves,
+                name="hand_down",
+            )
+            back[i] = swapped(send, level_num)
+    key_grads, value_grads = [], []
+    for i in range(N_PARTS):
+        send_k, send_v, total_k, total_v = near_call(
+            leaf_kernel,
+            place,
+            (held[i], back[i]) + tuple(partial_grads[i][1:5]),
+            [(tall, BF16), (tall, BF16), (tall, F32), (tall, F32)],
+            scratch=halves,
+            name="hand_down_leaf",
+        )
+        key_grads.append((total_k + swapped(send_k, 0).astype(F32)).astype(BF16))
+        value_grads.append((total_v + swapped(send_v, 0).astype(F32)).astype(BF16))
+    context = jnp.concatenate(contexts, axis=1)
+    key_grad = jnp.concatenate(key_grads, axis=1)
+    value_grad = jnp.concatenate(value_grads, axis=1)
     return context[None], query_grad[None], key_grad[None], value_grad[None], weight_grad
+
+
+def scatter_sum(weight_term, seq_count):
+    groups = [list(range(core, seq_count, 2)) for core in range(2)]
+    return lax.psum_scatter(weight_term, "seq", scatter_dimension=0, axis_index_groups=groups, tiled=False)
 
 
 def solution(mesh):

time: 176 us -> 183 us (1.040)
  waiting for transfers between devices: 76.7 us -> 28.3 us
  starting transfers between devices: 19.4 us -> 48.6 us
  local copies, waits for them, and re-layouts: 8.99 us -> 34.9 us
    ppermute x17 -> x35, waiting for transfers between devices: 61.7 us -> 14.7 us  [swapped(): lax.ppermute(value, 'seq', [(i, i ^ HOPS[level_num]) for i in range(count)])]
    unnamed x37 -> x146, local copies, waits for them, and re-layouts: 7.51 us -> 34.3 us
    ppermute x17 -> x35, starting transfers between devices: 19.3 us -> 36.3 us  [swapped(): lax.ppermute(value, 'seq', [(i, i ^ HOPS[level_num]) for i in range(count)])]
    reduce_scatter x1 -> x0, waiting for transfers between devices: 14.2 us -> none  [local(): lax.psum_scatter(weight_term, 'seq', scatter_dimension=0, tiled=True)]
    ppermute x0 -> x7, waiting for transfers between devices: none -> 12.9 us  [the longest x4 12.9 us: ring_gather(): from_below = lax.ppermute(from_below, axis, up)]
    ppermute x0 -> x7, starting transfers between devices: none -> 12.2 us  [the longest x3 9.63 us: ring_gather(): from_above = lax.ppermute(from_above, axis, down)]
    broadcast_in_dim x0 -> x2, other arithmetic: none -> 2.41 us  [the longest x1 1.69 us: local(): query_grad[None]]
    pallas_call x12 -> x23, Pallas kernels: 49.1 us -> 48.5 us  [the longest x17 20 us: near_call(): pl.pallas_call(kernel, in_specs=[SMEM] + [VMEM] * len(args), out_specs=[V...]
  transfers between devices with their start and end apart: 19 -> 43, of which waited for: 13 -> 10; matrix products, arithmetic and copies ran while one was open for 5% -> 4% of each run, Pallas kernels for 24% -> 24%
where the time goes in v1:
time: 183 us; the launch traced here: 181 us
  starting transfers between devices  48.6 us (27%)
  Pallas kernels  48.5 us (27%)
  local copies, waits for them, and re-layouts  34.9 us (19%)
  waiting for transfers between devices  28.3 us (15%)
  between operations  14.6 us (8%)
  other arithmetic  6.01 us (3%)
    ppermute x35, starting transfers between devices, swapped(): lax.ppermute(value, 'seq', [(i, i ^ HOPS[level_num]) for i in range(count)])  36.3 us
    unnamed x146, local copies, waits for them, and re-layouts  34.3 us
    pallas_call x17, Pallas kernels, near_call(): pl.pallas_call(kernel, in_specs=[SMEM] + [VMEM] * len(args), out_specs=[V...  20 us
    ppermute x35, waiting for transfers between devices, swapped(): lax.ppermute(value, 'seq', [(i, i ^ HOPS[level_num]) for i in range(count)])  14.7 us
    ppermute x4, waiting for transfers between devices, ring_gather(): from_below = lax.ppermute(from_below, axis, up)  12.9 us
    ppermute x3, starting transfers between devices, ring_gather(): from_above = lax.ppermute(from_above, axis, down)  9.63 us
    pallas_call x2, Pallas kernels, local(): pl.pallas_call(functools.partial(backward_kernel, scaling, n_up), grid=(p...  9.55 us
    pallas_call x2, Pallas kernels, local(): pl.pallas_call(functools.partial(forward_kernel, scaling, n_up), grid=(pa...  9.15 us
  transfers between devices with their start and end apart: 43, of which 10 were waited for; matrix products, arithmetic and copies ran while one was open for 4% of the time, Pallas kernels for 24%

profile of v1, /device:TPU:1, one launch (start us, length us, event | category | flops | bytes accessed | tf_op | source)
XLA Modules:
  0.0 180.9 jit_solution(14341243420595459670)
XLA Ops:
  7.2 2.5 %collective-permute-start.18 = (bf16[256,512]{1,0:T(8,128)(2,1)}, bf16[256,512]{1,0:T(8,128)(2,1)S(1)}, u32[]{:S(2)}, u32[]{:S(2)}) collective-permute-start(bf16[256,512]{1,0:T(8,128)(2,1)} %bitcast.30), channel_id=1, source_target_pairs={{0,1},{1,2},{2,3},{3,4},{4,5},{5,6},{6,7},{7,0},{8,9},{9,10},{10,1... | collective-permute-start | bytes 786440 | tf_op jit(solution)/shard_map/ppermute | solution.py:256
  9.8 4.0 %collective-permute-start.19 = (bf16[256,512]{1,0:T(8,128)(2,1)}, bf16[256,512]{1,0:T(8,128)(2,1)S(1)}, u32[]{:S(2)}, u32[]{:S(2)}) collective-permute-start(bf16[256,512]{1,0:T(8,128)(2,1)} %bitcast.31), channel_id=1, source_target_pairs={{0,7},{1,0},{2,1},{3,2},{4,3},{5,4},{6,5},{7,6},{8,15},{9,8},{10,9... | collective-permute-start | bytes 786440 | tf_op jit(solution)/shard_map/ppermute | solution.py:259
  13.8 6.2 %collective-permute-done.18.refs_1_ = bf16[256,512]{1,0:T(8,128)(2,1)S(1)} collective-permute-done((bf16[256,512]{1,0:T(8,128)(2,1)}, bf16[256,512]{1,0:T(8,128)(2,1)S(1)}, u32[]{:S(2)}, u32[]{:S(2)}) %collective-permute-start.18) | collective-permute-done | bytes 262176 | tf_op jit(solution)/shard_map/ppermute | solution.py:256
  20.0 2.7 %collective-permute-start.21 = (bf16[256,512]{1,0:T(8,128)(2,1)S(1)}, bf16[256,512]{1,0:T(8,128)(2,1)S(1)}, u32[]{:S(2)}, u32[]{:S(2)}) collective-permute-start(bf16[256,512]{1,0:T(8,128)(2,1)S(1)} %collective-permute-done.19.refs_2_), channel_id=1, source_target_pairs={{0,7},{1,0},{2,1},{3,2},{4,3},{5,4},{6,5},{7,6},{8,15},{9,8},{10,9... | collective-permute-start | bytes 786440 | tf_op jit(solution)/shard_map/ppermute | solution.py:259
  22.6 5.1 %collective-permute-done.20.refs_3_ = bf16[256,512]{1,0:T(8,128)(2,1)S(1)} collective-permute-done((bf16[256,512]{1,0:T(8,128)(2,1)S(1)}, bf16[256,512]{1,0:T(8,128)(2,1)S(1)}, u32[]{:S(2)}, u32[]{:S(2)}) %collective-permute-start.20) | collective-permute-done | bytes 262176 | tf_op jit(solution)/shard_map/ppermute | solution.py:256
  27.7 2.2 %collective-permute-start = (bf16[256,512]{1,0:T(8,128)(2,1)}, bf16[256,512]{1,0:T(8,128)(2,1)S(1)}, u32[]{:S(2)}, u32[]{:S(2)}) collective-permute-start(bf16[256,512]{1,0:T(8,128)(2,1)} %bitcast.18), channel_id=1, source_target_pairs={{0,8},{8,0},{16,24},{24,16},{32,40},{40,32},{48,56},{56,48},{64,72... | collective-permute-start | bytes 786440 | tf_op jit(solution)/shard_map/ppermute | solution.py:19
  30.0 2.9 %collective-permute-start.23 = (bf16[256,512]{1,0:T(8,128)(2,1)S(1)}, bf16[256,512]{1,0:T(8,128)(2,1)S(1)}, u32[]{:S(2)}, u32[]{:S(2)}) collective-permute-start(bf16[256,512]{1,0:T(8,128)(2,1)S(1)} %collective-permute-done.21.refs_4_), channel_id=1, source_target_pairs={{0,7},{1,0},{2,1},{3,2},{4,3},{5,4},{6,5},{7,6},{8,15},{9,8},{10,9... | collective-permute-start | bytes 786440 | tf_op jit(solution)/shard_map/ppermute | solution.py:259
  39.7 2.6 %collective-permute-done.10.other_ref.refs_4_ = bf16[256,256]{1,0:T(8,128)(2,1)S(1)} collective-permute-done((bf16[256,256]{1,0:T(8,128)(2,1)S(1)}, bf16[256,256]{1,0:T(8,128)(2,1)S(1)}, u32[]{:S(2)}, u32[]{:S(2)}) %collective-permute-start.10) | collective-permute-done | bytes 131104 | tf_op jit(solution)/shard_map/ppermute | solution.py:19
  43.2 2.8 %collective-permute-start.11 = (bf16[256,256]{1,0:T(8,128)(2,1)S(1)}, bf16[256,256]{1,0:T(8,128)(2,1)S(1)}, u32[]{:S(2)}, u32[]{:S(2)}) collective-permute-start(bf16[256,256]{1,0:T(8,128)(2,1)S(1)} %pool_group.9.mine_ref), channel_id=1, source_target_pairs={{0,48},{8,56},{16,32},{24,40},{32,16},{40,24},{48,0},{56,8},{64,11... | collective-permute-start | bytes 393224 | tf_op jit(solution)/shard_map/ppermute | solution.py:19
  47.5 5.1 %context_grad.1 = (bf16[256,512]{1,0:T(8,128)(2,1)}, bf16[8,256,256]{2,1,0:T(8,128)(2,1)}) custom-call(s32[2]{0:T(128)} %pad_add_fusion.place_ref, bf16[512,4096]{1,0:T(8,128)(2,1)} %weight_ref.1, bf16[256,512]{1,0:T(8,128)(2,1)} %bitcast.32, bf16[256,512]{1,0:T(8,128)(2,1)} %copy-done.50, bf16[256,512]{1,0:T(8,128)(2,1)} %copy-done.51, ...), custom_call_target="tpu_custom_call" | custom-call | tf_op jit(solution)/shard_map/context_grad/pallas_call | solution.py:302
  52.6 4.3 %collective-permute-start.39 = (bf16[8,256,256]{2,1,0:T(8,128)(2,1)}, bf16[8,256,256]{2,1,0:T(8,128)(2,1)S(1)}, u32[]{:S(2)}, u32[]{:S(2)}) collective-permute-start(bf16[8,256,256]{2,1,0:T(8,128)(2,1)} %get-tuple-element.96), channel_id=1, source_target_pairs={{0,8},{8,0},{16,24},{24,16},{32,40},{40,32},{48,56},{56,48},{64,72... | collective-permute-start | bytes 3145736 | tf_op jit(solution)/shard_map/ppermute | solution.py:19
  60.9 3.3 %collective-permute-done.3.other_ref.refs_5_ = bf16[256,256]{1,0:T(8,128)(2,1)S(1)} collective-permute-done((bf16[256,256]{1,0:T(8,128)(2,1)S(1)}, bf16[256,256]{1,0:T(8,128)(2,1)S(1)}, u32[]{:S(2)}, u32[]{:S(2)}) %collective-permute-start.3) | collective-permute-done | bytes 131104 | tf_op jit(solution)/shard_map/ppermute | solution.py:19
  67.2 1.9 %collective-permute-start.13 = (bf16[256,256]{1,0:T(8,128)(2,1)S(1)}, bf16[256,256]{1,0:T(8,128)(2,1)S(1)}, u32[]{:S(2)}, u32[]{:S(2)}) collective-permute-start(bf16[256,256]{1,0:T(8,128)(2,1)S(1)} %pool_group.11), channel_id=1, source_target_pairs={{0,192},{8,200},{16,208},{24,216},{32,224},{40,232},{48,240},{56,2... | collective-permute-start | bytes 393224 | tf_op jit(solution)/shard_map/ppermute | solution.py:19
  72.9 1.8 collective-permute-start.16
  75.5 2.9 %collective-permute-done.5.refs_7_ = bf16[256,256]{1,0:T(8,128)(2,1)S(1)} collective-permute-done((bf16[256,256]{1,0:T(8,128)(2,1)S(1)}, bf16[256,256]{1,0:T(8,128)(2,1)S(1)}, u32[]{:S(2)}, u32[]{:S(2)}) %collective-permute-start.5) | collective-permute-done | bytes 131104 | tf_op jit(solution)/shard_map/ppermute | solution.py:19
  81.0 4.7 %attention_forward.3 = (bf16[256,256]{1,0:T(8,128)(2,1)}, bf16[2,256,1536]{2,1,0:T(8,128)(2,1)}, bf16[1536,256]{1,0:T(8,128)(2,1)}, bf16[1536,256]{1,0:T(8,128)(2,1)}) custom-call(s32[2]{0:T(128)} %pad_add_fusion.place_ref, f32[1,1536]{1,0:T(1,128)} %select_n.33.weight_ref, bf16[256,512]{1,0:T(8,128)(2,1)} %bitcast.26, bf16[256,512]{1,0:T(8,128)(2,1)} %bitcast.19, ...), custom_call_target="tpu_custom_call" | custom-call | tf_op jit(solution)/shard_map/attention_forward/pallas_call | solution.py:325
  87.3 4.5 %attention_forward.2 = (bf16[256,256]{1,0:T(8,128)(2,1)}, bf16[2,256,1536]{2,1,0:T(8,128)(2,1)}, bf16[1536,256]{1,0:T(8,128)(2,1)}, bf16[1536,256]{1,0:T(8,128)(2,1)}) custom-call(s32[2]{0:T(128)} %pad_add_fusion.place_ref, f32[1,1536]{1,0:T(1,128)} %select_n.33.weight_ref, bf16[256,512]{1,0:T(8,128)(2,1)} %bitcast.27, bf16[256,512]{1,0:T(8,128)(2,1)} %bitcast.20, ...), custom_call_target="tpu_custom_call" | custom-call | tf_op jit(solution)/shard_map/attention_forward/pallas_call | solution.py:325
  95.1 4.7 %weight_term.1 = bf16[16,512,128]{2,1,0:T(8,128)(2,1)} custom-call(s32[2]{0:T(128)} %pad_add_fusion.place_ref, bf16[256,512]{1,0:T(8,128)(2,1)} %bitcast.33, bf16[256,512]{1,0:T(8,128)(2,1)} %copy-done.50, bf16[256,512]{1,0:T(8,128)(2,1)} %copy-done.51, bf16[256,512]{1,0:T(8,128)(2,1)} %copy-done.52, bf16[256,512]{1,0:T(8,128)(2,1)} %copy-done.53, ...), custom_call_target="tpu_custom_call" | custom-call | tf_op jit(solution)/shard_map/weight_term/pallas_call | solution.py:344
  99.8 4.7 %attention_backward.3 = (bf16[256,256]{1,0:T(8,128)(2,1)}, f32[256,256]{1,0:T(8,128)}, f32[256,256]{1,0:T(8,128)}, f32[256,256]{1,0:T(8,128)}, f32[256,256]{1,0:...) custom-call(s32[2]{0:T(128)} %pad_add_fusion.place_ref, bf16[256,512]{1,0:T(8,128)(2,1)} %bitcast.28, ...), custom_call_target="tpu_custom_call" | custom-call | tf_op jit(solution)/shard_map/attention_backward/pallas_call | solution.py:358
  105.2 4.8 %attention_backward.2 = (bf16[256,256]{1,0:T(8,128)(2,1)}, f32[256,256]{1,0:T(8,128)}, f32[256,256]{1,0:T(8,128)}, f32[256,256]{1,0:T(8,128)}, f32[256,256]{1,0:...) custom-call(s32[2]{0:T(128)} %pad_add_fusion.place_ref, bf16[256,512]{1,0:T(8,128)(2,1)} %bitcast.29, ...), custom_call_target="tpu_custom_call" | custom-call | tf_op jit(solution)/shard_map/attention_backward/pallas_call | solution.py:358
  115.4 3.7 %collective-permute-done.32.back_ref = bf16[256,256]{1,0:T(8,128)(2,1)S(1)} collective-permute-done((bf16[256,256]{1,0:T(8,128)(2,1)S(1)}, bf16[256,256]{1,0:T(8,128)(2,1)S(1)}, u32[]{:S(2)}, u32[]{:S(2)}) %collective-permute-start.32) | collective-permute-done | bytes 131104 | tf_op jit(solution)/shard_map/ppermute | solution.py:19
  138.2 2.2 %collective-permute-start.28 = (bf16[256,256]{1,0:T(8,128)(2,1)}, bf16[256,256]{1,0:T(8,128)(2,1)S(1)}, u32[]{:S(2)}, u32[]{:S(2)}) collective-permute-start(bf16[256,256]{1,0:T(8,128)(2,1)} %get-tuple-element.68), channel_id=1, source_target_pairs={{0,48},{8,56},{16,32},{24,40},{32,16},{40,24},{48,0},{56,8},{64,11... | collective-permute-start | bytes 393224 | tf_op jit(solution)/shard_map/ppermute | solution.py:19
  142.4 1.9 %hand_down.11 = (bf16[256,256]{1,0:T(8,128)(2,1)}, f32[256,256]{1,0:T(8,128)S(1)}) custom-call(s32[2]{0:T(128)} %pad_add_fusion.place_ref, f32[4,256,256]{2,1,0:T(8,128)S(1)} %copy-done, bf16[4,256,256]{2,1,0:T(8,128)(2,1)S(1)} %copy-done.5, bf16[256,256]{1,0:T(8,128)(2,1)} %collective-permute-done.34.back_ref, f32[256,256]{1,0:T(8,128)S(1)} %copy-done.23), custom_call_target="tpu_custom_call" | custom-call | tf_op jit(solution)/shard_map/hand_down/pallas_call | solution.py:71
  160.0 3.4 %collective-permute-start.36 = (bf16[256,256]{1,0:T(8,128)(2,1)}, bf16[256,256]{1,0:T(8,128)(2,1)S(1)}, u32[]{:S(2)}, u32[]{:S(2)}) collective-permute-start(bf16[256,256]{1,0:T(8,128)(2,1)} %get-tuple-element.91), channel_id=1, source_target_pairs={{0,8},{8,0},{16,24},{24,16},{32,40},{40,32},{48,56},{56,48},{64,72... | collective-permute-start | bytes 393224 | tf_op jit(solution)/shard_map/ppermute | solution.py:19
  (250 shorter events, 81.3 us)
Async XLA Ops:
  7.2 166.9 %reduce-scatter.4.cloned.1.call-start = ((), (), s32[]{:S(2)}) async-start(), calls=%async_computation.1 | async-start | bytes 2228224
  7.2 12.7 %collective-permute-start.18 = (bf16[256,512]{1,0:T(8,128)(2,1)}, bf16[256,512]{1,0:T(8,128)(2,1)S(1)}, u32[]{:S(2)}, u32[]{:S(2)}) collective-permute-start(bf16[256,512]{1,0:T(8,128)(2,1)} %bitcast.30), channel_id=1, source_target_pairs={{0,1},{1,2},{2,3},{3,4},{4,5},{5,6},{6,7},{7,0},{8,9},{9,10},{10,1... | collective-permute-start | bytes 786440 | tf_op jit(solution)/shard_map/ppermute | solution.py:256
  9.8 10.2 %collective-permute-start.19 = (bf16[256,512]{1,0:T(8,128)(2,1)}, bf16[256,512]{1,0:T(8,128)(2,1)S(1)}, u32[]{:S(2)}, u32[]{:S(2)}) collective-permute-start(bf16[256,512]{1,0:T(8,128)(2,1)} %bitcast.31), channel_id=1, source_target_pairs={{0,7},{1,0},{2,1},{3,2},{4,3},{5,4},{6,5},{7,6},{8,15},{9,8},{10,9... | collective-permute-start | bytes 786440 | tf_op jit(solution)/shard_map/ppermute | solution.py:259
  19.9 7.8 %collective-permute-start.20 = (bf16[256,512]{1,0:T(8,128)(2,1)S(1)}, bf16[256,512]{1,0:T(8,128)(2,1)S(1)}, u32[]{:S(2)}, u32[]{:S(2)}) collective-permute-start(bf16[256,512]{1,0:T(8,128)(2,1)S(1)} %collective-permute-done.18.refs_1_), channel_id=1, source_target_pairs={{0,1},{1,2},{2,3},{3,4},{4,5},{5,6},{6,7},{7,0},{8,9},{9,10},{10,1... | collective-permute-start | bytes 786440 | tf_op jit(solution)/shard_map/ppermute | solution.py:256
  20.0 10.0 %collective-permute-start.21 = (bf16[256,512]{1,0:T(8,128)(2,1)S(1)}, bf16[256,512]{1,0:T(8,128)(2,1)S(1)}, u32[]{:S(2)}, u32[]{:S(2)}) collective-permute-start(bf16[256,512]{1,0:T(8,128)(2,1)S(1)} %collective-permute-done.19.refs_2_), channel_id=1, source_target_pairs={{0,7},{1,0},{2,1},{3,2},{4,3},{5,4},{6,5},{7,6},{8,15},{9,8},{10,9... | collective-permute-start | bytes 786440 | tf_op jit(solution)/shard_map/ppermute | solution.py:259
  27.7 6.9 %collective-permute-start.22 = (bf16[256,512]{1,0:T(8,128)(2,1)S(1)}, bf16[256,512]{1,0:T(8,128)(2,1)S(1)}, u32[]{:S(2)}, u32[]{:S(2)}) collective-permute-start(bf16[256,512]{1,0:T(8,128)(2,1)S(1)} %collective-permute-done.20.refs_3_), channel_id=1, source_target_pairs={{0,1},{1,2},{2,3},{3,4},{4,5},{5,6},{6,7},{7,0},{8,9},{9,10},{10,1... | collective-permute-start | bytes 786440 | tf_op jit(solution)/shard_map/ppermute | solution.py:256
  27.7 7.5 %collective-permute-start = (bf16[256,512]{1,0:T(8,128)(2,1)}, bf16[256,512]{1,0:T(8,128)(2,1)S(1)}, u32[]{:S(2)}, u32[]{:S(2)}) collective-permute-start(bf16[256,512]{1,0:T(8,128)(2,1)} %bitcast.18), channel_id=1, source_target_pairs={{0,8},{8,0},{16,24},{24,16},{32,40},{40,32},{48,56},{56,48},{64,72... | collective-permute-start | bytes 786440 | tf_op jit(solution)/shard_map/ppermute | solution.py:19
  30.0 16.1 %collective-permute-start.23 = (bf16[256,512]{1,0:T(8,128)(2,1)S(1)}, bf16[256,512]{1,0:T(8,128)(2,1)S(1)}, u32[]{:S(2)}, u32[]{:S(2)}) collective-permute-start(bf16[256,512]{1,0:T(8,128)(2,1)S(1)} %collective-permute-done.21.refs_4_), channel_id=1, source_target_pairs={{0,7},{1,0},{2,1},{3,2},{4,3},{5,4},{6,5},{7,6},{8,15},{9,8},{10,9... | collective-permute-start | bytes 786440 | tf_op jit(solution)/shard_map/ppermute | solution.py:259
  34.6 11.5 %collective-permute-start.24 = (bf16[256,512]{1,0:T(8,128)(2,1)S(1)}, bf16[256,512]{1,0:T(8,128)(2,1)S(1)}, u32[]{:S(2)}, u32[]{:S(2)}) collective-permute-start(bf16[256,512]{1,0:T(8,128)(2,1)S(1)} %collective-permute-done.22.refs_5_), channel_id=1, source_target_pairs={{0,1},{1,2},{2,3},{3,4},{4,5},{5,6},{6,7},{7,0},{8,9},{9,10},{10,1... | collective-permute-start | bytes 786440 | tf_op jit(solution)/shard_map/ppermute | solution.py:256
  39.5 17.4 %collective-permute-start.2 = (bf16[256,256]{1,0:T(8,128)(2,1)S(1)}, bf16[256,256]{1,0:T(8,128)(2,1)S(1)}, u32[]{:S(2)}, u32[]{:S(2)}) collective-permute-start(bf16[256,256]{1,0:T(8,128)(2,1)S(1)} %get-tuple-element.51.mine_ref), channel_id=1, source_target_pairs={{0,16},{8,24},{16,0},{24,8},{32,48},{40,56},{48,32},{56,40},{64,80... | collective-permute-start | bytes 393224 | tf_op jit(solution)/shard_map/ppermute | solution.py:19
  43.2 14.7 %collective-permute-start.11 = (bf16[256,256]{1,0:T(8,128)(2,1)S(1)}, bf16[256,256]{1,0:T(8,128)(2,1)S(1)}, u32[]{:S(2)}, u32[]{:S(2)}) collective-permute-start(bf16[256,256]{1,0:T(8,128)(2,1)S(1)} %pool_group.9.mine_ref), channel_id=1, source_target_pairs={{0,48},{8,56},{16,32},{24,40},{32,16},{40,24},{48,0},{56,8},{64,11... | collective-permute-start | bytes 393224 | tf_op jit(solution)/shard_map/ppermute | solution.py:19
  52.6 40.9 %collective-permute-start.39 = (bf16[8,256,256]{2,1,0:T(8,128)(2,1)}, bf16[8,256,256]{2,1,0:T(8,128)(2,1)S(1)}, u32[]{:S(2)}, u32[]{:S(2)}) collective-permute-start(bf16[8,256,256]{2,1,0:T(8,128)(2,1)} %get-tuple-element.96), channel_id=1, source_target_pairs={{0,8},{8,0},{16,24},{24,16},{32,40},{40,32},{48,56},{56,48},{64,72... | collective-permute-start | bytes 3145736 | tf_op jit(solution)/shard_map/ppermute | solution.py:19
  58.8 7.6 %collective-permute-start.12 = (bf16[256,256]{1,0:T(8,128)(2,1)S(1)}, bf16[256,256]{1,0:T(8,128)(2,1)S(1)}, u32[]{:S(2)}, u32[]{:S(2)}) collective-permute-start(bf16[256,256]{1,0:T(8,128)(2,1)S(1)} %pool_group.10.mine_ref), channel_id=1, source_target_pairs={{0,64},{8,72},{16,80},{24,88},{32,96},{40,104},{48,112},{56,120},{... | collective-permute-start | bytes 393224 | tf_op jit(solution)/shard_map/ppermute | solution.py:19
  60.1 12.9 %collective-permute-start.14 = (bf16[256,256]{1,0:T(8,128)(2,1)S(1)}, bf16[256,256]{1,0:T(8,128)(2,1)S(1)}, u32[]{:S(2)}, u32[]{:S(2)}) collective-permute-start(bf16[256,256]{1,0:T(8,128)(2,1)S(1)} %collective-permute-done.10.other_ref.refs_4_), channel_id=1, source_target_pairs={{0,8},{8,0},{16,24},{24,16},{32,40},{40,32},{48,56},{56,48},{64,72... | collective-permute-start | bytes 393224 | tf_op jit(solution)/shard_map/ppermute | solution.py:19
  67.2 7.6 %collective-permute-start.13 = (bf16[256,256]{1,0:T(8,128)(2,1)S(1)}, bf16[256,256]{1,0:T(8,128)(2,1)S(1)}, u32[]{:S(2)}, u32[]{:S(2)}) collective-permute-start(bf16[256,256]{1,0:T(8,128)(2,1)S(1)} %pool_group.11), channel_id=1, source_target_pairs={{0,192},{8,200},{16,208},{24,216},{32,224},{40,232},{48,240},{56,2... | collective-permute-start | bytes 393224 | tf_op jit(solution)/shard_map/ppermute | solution.py:19
  75.0 10.7 %collective-permute-start.6 = (bf16[256,256]{1,0:T(8,128)(2,1)S(1)}, bf16[256,256]{1,0:T(8,128)(2,1)S(1)}, u32[]{:S(2)}, u32[]{:S(2)}) collective-permute-start(bf16[256,256]{1,0:T(8,128)(2,1)S(1)} %collective-permute-done.2.other_ref.refs_4_), channel_id=1, source_target_pairs={{0,8},{8,0},{16,24},{24,16},{32,40},{40,32},{48,56},{56,48},{64,72... | collective-permute-start | bytes 393224 | tf_op jit(solution)/shard_map/ppermute | solution.py:19
  78.4 7.5 %collective-permute-start.7 = (bf16[256,256]{1,0:T(8,128)(2,1)S(1)}, bf16[256,256]{1,0:T(8,128)(2,1)S(1)}, u32[]{:S(2)}, u32[]{:S(2)}) collective-permute-start(bf16[256,256]{1,0:T(8,128)(2,1)S(1)} %collective-permute-done.3.other_ref.refs_5_), channel_id=1, source_target_pairs={{0,8},{8,0},{16,24},{24,16},{32,40},{40,32},{48,56},{56,48},{64,72... | collective-permute-start | bytes 393224 | tf_op jit(solution)/shard_map/ppermute | solution.py:19
  111.9 7.2 %collective-permute-start.32 = (bf16[256,256]{1,0:T(8,128)(2,1)S(1)}, bf16[256,256]{1,0:T(8,128)(2,1)S(1)}, u32[]{:S(2)}, u32[]{:S(2)}) collective-permute-start(bf16[256,256]{1,0:T(8,128)(2,1)S(1)} %hand_down_top.3), channel_id=1, source_target_pairs={{0,192},{8,200},{16,208},{24,216},{32,224},{40,232},{48,240},{56,2... | collective-permute-start | bytes 393224 | tf_op jit(solution)/shard_map/ppermute | solution.py:19
  114.0 8.5 %collective-permute-start.26 = (bf16[256,256]{1,0:T(8,128)(2,1)S(1)}, bf16[256,256]{1,0:T(8,128)(2,1)S(1)}, u32[]{:S(2)}, u32[]{:S(2)}) collective-permute-start(bf16[256,256]{1,0:T(8,128)(2,1)S(1)} %hand_down_top.2), channel_id=1, source_target_pairs={{0,192},{8,200},{16,208},{24,216},{32,224},{40,232},{48,240},{56,2... | collective-permute-start | bytes 393224 | tf_op jit(solution)/shard_map/ppermute | solution.py:19
  126.0 7.9 %collective-permute-start.27 = (bf16[256,256]{1,0:T(8,128)(2,1)}, bf16[256,256]{1,0:T(8,128)(2,1)S(1)}, u32[]{:S(2)}, u32[]{:S(2)}) collective-permute-start(bf16[256,256]{1,0:T(8,128)(2,1)} %get-tuple-element.66), channel_id=1, source_target_pairs={{0,64},{8,72},{16,80},{24,88},{32,96},{40,104},{48,112},{56,120},{... | collective-permute-start | bytes 393224 | tf_op jit(solution)/shard_map/ppermute | solution.py:19
  133.4 7.1 %collective-permute-start.34 = (bf16[256,256]{1,0:T(8,128)(2,1)}, bf16[256,256]{1,0:T(8,128)(2,1)}, u32[]{:S(2)}, u32[]{:S(2)}) collective-permute-start(bf16[256,256]{1,0:T(8,128)(2,1)} %get-tuple-element.82), channel_id=1, source_target_pairs={{0,48},{8,56},{16,32},{24,40},{32,16},{40,24},{48,0},{56,8},{64,11... | collective-permute-start | bytes 393224 | tf_op jit(solution)/shard_map/ppermute | solution.py:19
  145.0 6.9 %collective-permute-start.35 = (bf16[256,256]{1,0:T(8,128)(2,1)}, bf16[256,256]{1,0:T(8,128)(2,1)S(1)}, u32[]{:S(2)}, u32[]{:S(2)}) collective-permute-start(bf16[256,256]{1,0:T(8,128)(2,1)} %get-tuple-element.85), channel_id=1, source_target_pairs={{0,16},{8,24},{16,0},{24,8},{32,48},{40,56},{48,32},{56,40},{64,80... | collective-permute-start | bytes 393224 | tf_op jit(solution)/shard_map/ppermute | solution.py:19
  150.5 15.3 %collective-permute-start.29 = (bf16[256,256]{1,0:T(8,128)(2,1)S(1)}, bf16[256,256]{1,0:T(8,128)(2,1)S(1)}, u32[]{:S(2)}, u32[]{:S(2)}) collective-permute-start(bf16[256,256]{1,0:T(8,128)(2,1)S(1)} %get-tuple-element.71), channel_id=1, source_target_pairs={{0,16},{8,24},{16,0},{24,8},{32,48},{40,56},{48,32},{56,40},{64,80... | collective-permute-start | bytes 393224 | tf_op jit(solution)/shard_map/ppermute | solution.py:19
  160.0 11.0 %collective-permute-start.36 = (bf16[256,256]{1,0:T(8,128)(2,1)}, bf16[256,256]{1,0:T(8,128)(2,1)S(1)}, u32[]{:S(2)}, u32[]{:S(2)}) collective-permute-start(bf16[256,256]{1,0:T(8,128)(2,1)} %get-tuple-element.91), channel_id=1, source_target_pairs={{0,8},{8,0},{16,24},{24,16},{32,40},{40,32},{48,56},{56,48},{64,72... | collective-permute-start | bytes 393224 | tf_op jit(solution)/shard_map/ppermute | solution.py:19
  (91 other events, 566.2 us)
Sparse Core Ops, SparseCore 0:
  99.9 74.0 reduce-scatter.3
